TPU v7x, 128 devices: a whole 4x4x4 slice. The times are simulated.
128 devices in a mesh: req: 16 (over x, z), tp: 8 (over y, core).
Axes of the slice: x: 4, y: 4, z: 4, core: 2. Of those that a mesh axis runs over, the one named last changes fastest.
Arguments:
- hidden: bfloat16 [8192, 2048], P('req', 'tp'), may hold values from -6 to 6
- qkv_weight: bfloat16 [2048, 3072], P('req', 'tp'), may hold values from -0.125 to 0.125
- out_weight: bfloat16 [2048, 2048], P('tp', 'req'), may hold values from -0.125 to 0.125
- kv_pages: bfloat16 [1024, 128, 1024], P('req', None, 'tp'), may hold values from -160 to 160, as said below
- cache_pages: int32 [16], replicated, may hold values from 1 to 256, 960 in all
- slot_order: int32 [1024], replicated, may hold values from 0 to 1023, each once
Outputs:
- attention_out: bfloat16 [8192, 2048], P('req', 'tp')
- pages_out: bfloat16 [1024, 128, 1024], P('req', None, 'tp')
Inputs may be any that keep to these rules, and one draw needn't show every extreme that they name: `cache_pages`: each request has at least one cached page and at most 256, and one request has exactly 256; all cached pages plus 4 new pages per request fill exactly 1024 slots. `slot_order`: each global slot appears once. `kv_pages`: cached rotated keys and values.
All inputs are finite; a program needn't handle non-finite values.
Results may differ from a plain program's by a relative error of at most 0.02.
The roundings to bfloat16 on the way count: a program that leaves them out, or rounds other values in their place, can miss the bound.
Values may be sent and summed in bfloat16 or wider, within the bound.
A program may use at most 128 MiB of HBM per device.

v0:
```python
import math
import jax
import jax.numpy as jnp
from jax import lax
from jax.sharding import PartitionSpec as P

HD = 64
GROUP = 4
SPAN = 512
THETA = 1000000.0
NEG_BIG = -1e30


def rotary(values, positions):
    head_width = values.shape[-1]
    half_width = head_width // 2
    inv_freq = jnp.power(THETA, -(jnp.arange(half_width, dtype=jnp.float32) * 2.0 / head_width))
    angles = positions.astype(jnp.float32)[..., None] * inv_freq
    cosines = jnp.cos(angles)
    sines = jnp.sin(angles)
    lower_half = values[..., :half_width]
    upper_half = values[..., half_width:]
    return jnp.concatenate(
        [lower_half * cosines - upper_half * sines, upper_half * cosines + lower_half * sines],
        axis=-1,
    )


def to_columns(stat):
    return jnp.moveaxis(stat, -1, -3)[..., None]


def locate(slot_ids, cache_pages, slot_order, new_pages):
    requests = cache_pages.shape[0]
    slot_count = slot_order.shape[0]
    counts = cache_pages + new_pages
    page_ends = jnp.cumsum(counts)
    starts = page_ends - counts
    ranking = jnp.sum(
        jnp.where(
            slot_order[None, :] == slot_ids[:, None],
            jnp.arange(slot_count, dtype=jnp.int32)[None, :],
            0,
        ),
        axis=1,
    )
    holder = jnp.sum((starts[None, :] <= ranking[:, None]).astype(jnp.int32), axis=1) - 1
    onehot = jnp.arange(requests, dtype=jnp.int32)[None, :] == holder[:, None]
    first_page = jnp.sum(jnp.where(onehot, starts[None, :], 0), axis=1)
    cached = jnp.sum(jnp.where(onehot, cache_pages[None, :], 0), axis=1)
    return (holder, ranking - first_page, cached)


def write_pages(kv_pages, fresh, slot_req, page_index, cached, new_pages):
    page_rows = kv_pages.shape[1]
    lane_width = kv_pages.shape[2]
    fresh_pages = fresh.reshape(-1, page_rows, lane_width)
    pick = slot_req * new_pages + jnp.clip(page_index - cached, 0, new_pages - 1)
    return jnp.where((page_index >= cached)[:, None, None], fresh_pages[pick], kv_pages)


def block_terms(queries, query_start, page_block, slot_req, key_start, is_live):
    block_slots = page_block.shape[0]
    page_rows = page_block.shape[1]
    kv_heads = queries.shape[2]
    head_width = queries.shape[4]
    span_rows = queries.shape[1]
    kv_pairs = page_block.reshape(block_slots, page_rows, kv_heads, 2, head_width)
    key_rows = kv_pairs[:, :, :, 0, :]
    value_rows = kv_pairs[:, :, :, 1, :]
    chosen = queries[slot_req]
    scores = jnp.einsum(
        "bckgd,bpkd->bkgcp", chosen, key_rows, preferred_element_type=jnp.float32
    ) * (1.0 / math.sqrt(head_width))
    query_pos = query_start[slot_req][:, None] + jnp.arange(span_rows, dtype=jnp.int32)[None, :]
    key_pos = key_start[:, None] + jnp.arange(page_rows, dtype=jnp.int32)[None, :]
    visible = (key_pos[:, None, :] <= query_pos[:, :, None]) & is_live[:, None, None]
    visible = visible[:, None, None, :, :]
    masked = jnp.where(visible, scores, NEG_BIG)
    block_max = jnp.max(masked, axis=-1)
    exp_terms = jnp.where(visible, jnp.exp(masked - block_max[..., None]), 0.0)
    block_sum = jnp.sum(exp_terms, axis=-1)
    weights = exp_terms.astype(jnp.bfloat16)
    block_out = jnp.einsum(
        "bkgcp,bpkd->bckgd", weights, value_rows, preferred_element_type=jnp.float32
    )
    return (block_out, block_max, block_sum)


def fold(running, terms, slot_req):
    acc_out, acc_max, acc_sum = running
    block_out, block_max, block_sum = terms
    for j in range(block_out.shape[0]):
        target = slot_req[j]
        old_max = lax.dynamic_index_in_dim(acc_max, target, 0, keepdims=False)
        new_max = jnp.maximum(old_max, block_max[j])
        keep_old = jnp.exp(old_max - new_max)
        take_new = jnp.exp(block_max[j] - new_max)
        old_out = lax.dynamic_index_in_dim(acc_out, target, 0, keepdims=False)
        old_sum = lax.dynamic_index_in_dim(acc_sum, target, 0, keepdims=False)
        acc_out = lax.dynamic_update_index_in_dim(
            acc_out, old_out * to_columns(keep_old) + block_out[j] * to_columns(take_new), target, 0
        )
        acc_sum = lax.dynamic_update_index_in_dim(
            acc_sum, old_sum * keep_old + block_sum[j] * take_new, target, 0
        )
        acc_max = lax.dynamic_update_index_in_dim(acc_max, new_max, target, 0)
    return (acc_out, acc_max, acc_sum)


def init_state(requests, span_rows, kv_heads, group_size, head_width):
    return (
        jnp.zeros((requests, span_rows, kv_heads, group_size, head_width), jnp.float32),
        jnp.full((requests, kv_heads, group_size, span_rows), NEG_BIG, jnp.float32),
        jnp.zeros((requests, kv_heads, group_size, span_rows), jnp.float32),
    )


def body(hidden, qkv_weight, out_weight, kv_pages, cache_pages, slot_order):
    whole = lax.all_gather(hidden, "tp", axis=1, tiled=True)
    tok_rows = whole.shape[0]
    projected = jnp.dot(
        whole,
        lax.all_gather(qkv_weight, "req", axis=0, tiled=True),
        preferred_element_type=jnp.float32,
    )
    local_slots = kv_pages.shape[0]
    page_rows = kv_pages.shape[1]
    lane_width = kv_pages.shape[2]
    kv_heads = lane_width // (2 * HD)
    local_reqs = tok_rows // SPAN
    new_pages = SPAN // page_rows
    my_index = lax.axis_index("req")
    query_start = cache_pages * page_rows
    home_start = lax.dynamic_slice_in_dim(query_start, my_index * local_reqs, local_reqs, 0)
    projected = projected.reshape(local_reqs, SPAN, kv_heads, GROUP + 2, HD)
    positions = (home_start[:, None] + jnp.arange(SPAN, dtype=jnp.int32)[None, :])[:, :, None, None]
    queries = rotary(projected[:, :, :, :GROUP, :], positions).astype(jnp.bfloat16)
    key_new = rotary(projected[:, :, :, GROUP : GROUP + 1, :], positions).astype(jnp.bfloat16)
    value_new = projected[:, :, :, GROUP + 1 :, :].astype(jnp.bfloat16)
    fresh = jnp.concatenate([key_new, value_new], axis=3).reshape(local_reqs, SPAN, lane_width)
    my_slots = my_index * local_slots + jnp.arange(local_slots, dtype=jnp.int32)
    block_slots = math.gcd(local_slots, max(1, 512 // page_rows))
    fresh_all = lax.all_gather(fresh, "req", axis=0, tiled=True)
    slot_req, page_index, cached = locate(my_slots, cache_pages, slot_order, new_pages)
    pages_out = write_pages(kv_pages, fresh_all, slot_req, page_index, cached, new_pages)
    piece_pages = lax.all_gather(pages_out, "req", axis=0, tiled=True)
    piece_count = piece_pages.shape[0]
    piece_ids = jnp.arange(piece_count, dtype=jnp.int32)
    piece_req, piece_index, unused_cached = locate(piece_ids, cache_pages, slot_order, new_pages)
    local_req = piece_req - my_index * local_reqs
    is_mine = (local_req >= 0) & (local_req < local_reqs)
    ordering = jnp.argsort(jnp.where(is_mine, 0, 1).astype(jnp.int32), stable=True)
    ordering = jnp.concatenate([ordering, jnp.zeros((block_slots,), jnp.int32)])
    used_count = jnp.sum(is_mine.astype(jnp.int32))

    def advance(j, state_now):
        low_slot = j * block_slots
        picked = lax.dynamic_slice_in_dim(ordering, low_slot, block_slots, 0)
        page_block = piece_pages[picked]
        is_live = low_slot + jnp.arange(block_slots, dtype=jnp.int32) < used_count
        block_req = jnp.clip(local_req[picked], 0, local_reqs - 1)
        key_start = piece_index[picked] * page_rows
        terms = block_terms(queries, home_start, page_block, block_req, key_start, is_live)
        return fold(state_now, terms, block_req)

    acc_out, acc_max, acc_sum = lax.fori_loop(
        0,
        (used_count + block_slots - 1) // block_slots,
        advance,
        init_state(local_reqs, SPAN, kv_heads, GROUP, HD),
    )
    attention = acc_out / to_columns(acc_sum)
    attention_flat = attention.astype(jnp.bfloat16).reshape(tok_rows, kv_heads * GROUP * HD)
    head_terms = jnp.dot(
        attention_flat,
        lax.all_gather(out_weight, "req", axis=1, tiled=True),
        preferred_element_type=jnp.float32,
    )
    attention_out = lax.psum_scatter(
        head_terms.astype(jnp.bfloat16), "tp", scatter_dimension=1, tiled=True
    )
    return (attention_out, pages_out)


def solution(mesh):
    return jax.shard_map(
        body,
        mesh=mesh,
        in_specs=(P("req", "tp"), P("req", "tp"), P("tp", "req"), P("req", None, "tp"), P(), P()),
        out_specs=(P("req", "tp"), P("req", None, "tp")),
        check_vma=False,
    )
```

profile of v0, /device:TPU:0, one launch (start us, length us, event | category | flops | bytes accessed | tf_op | source)
XLA Modules:
  0.0 880.7 jit_solution(123321950454702308)
XLA Ops:
  11.6 45.0 %all-gather.8.cloned.1.call-done = bf16[2048,384]{1,0:T(8,128)(2,1)} async-done(((bf16[128,384]{1,0:T(8,128)(2,1)}), bf16[2048,384]{1,0:T(8,128)(2,1)}) %all-gather.8.cloned.1.call-update) | async-done | bytes 1572880 | tf_op jit(solution)/shard_map/all_gather | solution.py:124
  56.5 27.8 %all-gather.6.cloned.1.call-done = bf16[512,2048]{1,0:T(8,128)(2,1)} async-done(((bf16[512,256]{1,0:T(8,128)(2,1)}), bf16[512,2048]{1,0:T(8,128)(2,1)}) %all-gather.6.cloned.1.call-update) | async-done | bytes 2097168 | tf_op jit(solution)/shard_map/all_gather | solution.py:120
  84.3 3.1 fusion.54
  89.0 45.6 %all-gather.10.cloned.1.call-done = bf16[16,512,128]{2,1,0:T(8,128)(2,1)} async-done(((bf16[1,512,128]{2,1,0:T(8,128)(2,1)}), bf16[16,512,128]{2,1,0:T(8,128)(2,1)}) %all-gather.10.cloned.1.call-update) | async-done | bytes 2097168 | tf_op jit(solution)/shard_map/all_gather | solution.py:144
  134.6 2.5 gather_fusion.2
  137.1 3.2 broadcast_select_fusion
  143.2 4.4 sort.17
  147.8 189.2 %all-gather.12.cloned.1.call-done = bf16[1024,128,128]{2,1,0:T(8,128)(2,1)} async-done(((bf16[64,128,128]{2,1,0:T(8,128)(2,1)}), bf16[1024,128,128]{2,1,0:T(8,128)(2,1)}) %all-gather.12.cloned.1.call-update) | async-done | bytes 33554448 | tf_op jit(solution)/shard_map/all_gather | solution.py:147
  337.1 130.7 %while.15 = (s32[]{:T(128)}, f32[1,512,1,4,64]{1,4,3,0,2:T(8,128)S(1)}, f32[1,1,4,512]{3,2,1,0:T(4,128)S(1)}, f32[1,1,4,512]{3,2,1,0:T(4,128)S(1)}, s32[]{:T(128...) while((s32[]{:T(128)}, ...), condition=%wide.region_13.14_spmd.clone, body=%wide.region_10.13_spmd.clone.sunk | while | flops 284227616 | bytes 20279676 | solution.py:167
  339.4 1.4 gather_fusion.1
  341.8 1.2 fusion.68
  343.0 1.1 fusion.69
  347.0 1.4 gather_fusion.1
  349.5 1.2 fusion.68
  350.7 1.1 fusion.69
  354.7 1.4 gather_fusion.1
  357.2 1.2 fusion.68
  362.4 1.4 gather_fusion.1
  364.9 1.2 fusion.68
  370.1 1.4 gather_fusion.1
  372.5 1.2 fusion.68
  377.8 1.4 gather_fusion.1
  380.2 1.2 fusion.68
  385.5 1.4 gather_fusion.1
  387.9 1.2 fusion.68
  393.2 1.4 gather_fusion.1
  395.6 1.2 fusion.68
  400.8 1.4 gather_fusion.1
  403.3 1.2 fusion.68
  408.5 1.4 gather_fusion.1
  411.0 1.2 fusion.68
  416.2 1.4 gather_fusion.1
  418.7 1.2 fusion.68
  423.9 1.4 gather_fusion.1
  426.4 1.2 fusion.68
  431.6 1.4 gather_fusion.1
  434.0 1.2 fusion.68
  439.3 1.4 gather_fusion.1
  441.7 1.2 fusion.68
  447.0 1.4 gather_fusion.1
  449.4 1.2 fusion.68
  454.7 1.4 gather_fusion.1
  457.1 1.2 fusion.68
  462.4 1.4 gather_fusion.1
  464.8 1.2 fusion.68
  466.0 1.1 fusion.69
  467.8 3.3 convolution_convert_fusion
  471.2 402.6 %reduce-scatter.2.cloned.1.call-done = bf16[512,256]{1,0:T(8,128)(2,1)} async-done(((bf16[512,2048]{1,0:T(8,128)(2,1)}), bf16[512,256]{1,0:T(8,128)(2,1)}) %reduce-scatter.2.cloned.1.call-update) | async-done | bytes 262160 | tf_op jit(solution)/shard_map/reduce_scatter | solution.py:180
  (304 shorter events, 90.2 us)
Async XLA Ops:
  7.2 81.7 %copy-start.1 = (s32[16]{0:T(128)S(1)}, s32[16]{0:T(128)}, u32[]{:S(2)}) copy-start(s32[16]{0:T(128)} %param.12) | copy-start | bytes 196
  7.2 81.4 %copy-start = (s32[1024]{0:T(1024)S(1)}, s32[1024]{0:T(1024)}, u32[]{:S(2)}) copy-start(s32[1024]{0:T(1024)} %param.13) | copy-start | bytes 12292
  7.2 49.3 %all-gather.8.cloned.1.call-start = ((), (), s32[]{:S(2)}) async-start(), calls=%async_computation.2 | async-start | bytes 1671168 | tf_op jit(solution)/shard_map/all_gather | solution.py:124
  7.9 76.4 %all-gather.6.cloned.1.call-start = ((), (), s32[]{:S(2)}) async-start(), calls=%async_computation.1 | async-start | bytes 2359296 | tf_op jit(solution)/shard_map/all_gather | solution.py:120
  8.7 125.9 %all-gather.10.cloned.1.call-start = ((), (), s32[]{:S(2)}) async-start(), calls=%async_computation.3 | async-start | bytes 2228224 | tf_op jit(solution)/shard_map/all_gather | solution.py:144
  88.5 248.5 %all-gather.12.cloned.1.call-start = ((), (), s32[]{:S(2)}) async-start(), calls=%async_computation.4 | async-start | bytes 35651584 | tf_op jit(solution)/shard_map/all_gather | solution.py:147
  140.4 327.4 %all-gather.14.cloned.1.call-start = ((), (), s32[]{:S(2)}) async-start(), calls=%async_computation.5 | async-start | bytes 1114112 | tf_op jit(solution)/shard_map/all_gather | solution.py:177
  141.0 732.8 %reduce-scatter.2.cloned.1.call-start = ((), (), s32[]{:S(2)}) async-start(), calls=%async_computation.6 | async-start | bytes 2359296 | tf_op jit(solution)/shard_map/reduce_scatter | solution.py:180
Sparse Core Ops, SparseCore 0:
  10.2 46.2 all-gather.7
  58.2 26.0 all-gather.5
  88.6 45.9 all-gather.9
  140.5 196.4 all-gather.11
  338.9 42.8 all-gather.13
  471.3 402.4 reduce-scatter.1
where the time goes:
time: 887 us; the launch traced here: 881 us
  waiting for transfers between devices  712 us (80%)
  other arithmetic  68.7 us (8%)
  matrix products  43.1 us (5%)
  local copies, waits for them, and re-layouts  40.3 us (5%)
  between operations  14.9 us (2%)
    reduce_scatter x1, waiting for transfers between devices, body(): lax.psum_scatter(head_terms.astype(jnp.bfloat16), 'tp', scatter_dimension...  403 us
    all_gather x1, waiting for transfers between devices, body(): piece_pages = lax.all_gather(pages_out, 'req', axis=0, tiled=True)  189 us
    all_gather x1, waiting for transfers between devices, body(): fresh_all = lax.all_gather(fresh, 'req', axis=0, tiled=True)  45.6 us
    all_gather x1, waiting for transfers between devices, body(): lax.all_gather(qkv_weight, 'req', axis=0, tiled=True)  45 us
    all_gather x1, waiting for transfers between devices, body(): whole = lax.all_gather(hidden, 'tp', axis=1, tiled=True)  27.8 us
    gather x34, local copies, waits for them, and re-layouts, advance(): page_block = piece_pages[picked]  25.6 us
    dot_general x17, matrix products, block_terms(): jnp.einsum('bkgcp,bpkd->bckgd', weights, value_rows, preferred_element_ty...  21.1 us
    reduce_sum x17, other arithmetic, block_terms(): block_sum = jnp.sum(exp_terms, axis=-1)  18.6 us
  transfers between devices with their start and end apart: 6, of which 5 were waited for; matrix products, arithmetic and copies ran while one was open for 16% of the time, Pallas kernels for 0%

commit v1 on v0

--- a/solution.py
+++ b/solution.py
@@ -9,6 +9,17 @@
 SPAN = 512
 THETA = 1000000.0
 NEG_BIG = -1e30
+
+
+def orders_bind(inputs, peer_axis):
+    axis_len = lax.axis_size(peer_axis)
+    return lax.all_to_all(
+        jnp.tile(inputs, [axis_len if num == 0 else 1 for num in range(inputs.ndim)]),
+        axis_name=peer_axis,
+        split_axis=0,
+        concat_axis=0,
+        tiled=True,
+    )
 
 
 def rotary(values, positions):
@@ -119,11 +130,7 @@
 def body(hidden, qkv_weight, out_weight, kv_pages, cache_pages, slot_order):
     whole = lax.all_gather(hidden, "tp", axis=1, tiled=True)
     tok_rows = whole.shape[0]
-    projected = jnp.dot(
-        whole,
-        lax.all_gather(qkv_weight, "req", axis=0, tiled=True),
-        preferred_element_type=jnp.float32,
-    )
+    projected = jnp.dot(whole, orders_bind(qkv_weight, "req"), preferred_element_type=jnp.float32)
     local_slots = kv_pages.shape[0]
     page_rows = kv_pages.shape[1]
     lane_width = kv_pages.shape[2]

time: 887 us -> 844 us (0.952)
  waiting for transfers between devices: 712 us -> 659 us
    all_gather x1 -> x0, waiting for transfers between devices: 45 us -> none  [body(): lax.all_gather(qkv_weight, 'req', axis=0, tiled=True)]
    all_gather x1, waiting for transfers between devices: 27.8 us -> 0.02 us  [body(): whole = lax.all_gather(hidden, 'tp', axis=1, tiled=True)]
    all_to_all x0 -> x1, waiting for transfers between devices: none -> 22.2 us  [orders_bind(): lax.all_to_all(jnp.tile(inputs, [axis_len if num == 0 else 1 for num in r...]
  transfers between devices with their start and end apart: 6 -> 6, of which waited for: 5 -> 4; matrix products, arithmetic and copies ran while one was open for 16% -> 17% of each run, Pallas kernels for 0% -> 0%
where the time goes in v1:
time: 844 us; the launch traced here: 837 us
  waiting for transfers between devices  659 us (78%)
  other arithmetic  67.2 us (8%)
  local copies, waits for them, and re-layouts  44.4 us (5%)
  matrix products  42.8 us (5%)
  between operations  14.6 us (2%)
    reduce_scatter x1, waiting for transfers between devices, body(): lax.psum_scatter(head_terms.astype(jnp.bfloat16), 'tp', scatter_dimension...  403 us
    all_gather x1, waiting for transfers between devices, body(): piece_pages = lax.all_gather(pages_out, 'req', axis=0, tiled=True)  189 us
    all_gather x1, waiting for transfers between devices, body(): fresh_all = lax.all_gather(fresh, 'req', axis=0, tiled=True)  43.1 us
    gather x34, local copies, waits for them, and re-layouts, advance(): page_block = piece_pages[picked]  25.5 us
    all_to_all x1, waiting for transfers between devices, orders_bind(): lax.all_to_all(jnp.tile(inputs, [axis_len if num == 0 else 1 for num in r...  22.2 us
    dot_general x17, matrix products, block_terms(): jnp.einsum('bkgcp,bpkd->bckgd', weights, value_rows, preferred_element_ty...  20.9 us
    reduce_sum x17, other arithmetic, block_terms(): block_sum = jnp.sum(exp_terms, axis=-1)  18.5 us
  transfers between devices with their start and end apart: 6, of which 4 were waited for; matrix products, arithmetic and copies ran while one was open for 17% of the time, Pallas kernels for 0%

profile of v1, /device:TPU:0, one launch (start us, length us, event | category | flops | bytes accessed | tf_op | source)
XLA Modules:
  0.0 837.4 jit_solution(10830407321671779915)
XLA Ops:
  8.9 1.4 tile.2
  10.4 8.0 all-to-all-start
  20.0 22.2 %all-to-all-done = bf16[16,128,384]{1,2,0:T(8,128)(2,1)S(1)} async-done(((bf16[16,128,384]{1,2,0:T(8,128)(2,1)}), bf16[16,128,384]{1,2,0:T(8,128)(2,1)S(1)}, u32[]{:S(2)}, u32[]{:S(2)}) %all-to-all-start) | async-done | bytes 1572896 | tf_op jit(solution)/shard_map/all_to_all | solution.py:16
  43.8 2.6 fusion.47
  48.1 43.1 %all-gather.7.cloned.1.call-done = bf16[16,512,128]{2,1,0:T(8,128)(2,1)} async-done(((bf16[1,512,128]{2,1,0:T(8,128)(2,1)}), bf16[16,512,128]{2,1,0:T(8,128)(2,1)}) %all-gather.7.cloned.1.call-update) | async-done | bytes 2097168 | tf_op jit(solution)/shard_map/all_gather | solution.py:151
  91.1 2.5 gather_fusion.2
  93.7 3.2 broadcast_select_fusion
  99.7 4.4 sort.17
  104.3 189.2 %all-gather.9.cloned.1.call-done = bf16[1024,128,128]{2,1,0:T(8,128)(2,1)} async-done(((bf16[64,128,128]{2,1,0:T(8,128)(2,1)}), bf16[1024,128,128]{2,1,0:T(8,128)(2,1)}) %all-gather.9.cloned.1.call-update) | async-done | bytes 33554448 | tf_op jit(solution)/shard_map/all_gather | solution.py:154
  293.6 130.7 %while.15 = (s32[]{:T(128)}, f32[1,512,1,4,64]{1,4,3,0,2:T(8,128)S(1)}, f32[1,1,4,512]{3,2,1,0:T(4,128)S(1)}, f32[1,1,4,512]{3,2,1,0:T(4,128)S(1)}, s32[]{:T(128...) while((s32[]{:T(128)}, ...), condition=%wide.region_13.14_spmd.clone, body=%wide.region_10.13_spmd.clone.sunk | while | flops 284227616 | bytes 20279676 | solution.py:174
  295.9 1.4 gather_fusion.1
  298.3 1.2 fusion.71
  303.6 1.4 gather_fusion.1
  306.0 1.2 fusion.71
  311.2 1.4 gather_fusion.1
  313.7 1.2 fusion.71
  318.9 1.4 gather_fusion.1
  321.4 1.2 fusion.71
  322.6 1.1 fusion.72
  326.6 1.4 gather_fusion.1
  329.1 1.2 fusion.71
  330.3 1.1 fusion.72
  334.3 1.4 gather_fusion.1
  336.8 1.2 fusion.71
  342.0 1.4 gather_fusion.1
  344.5 1.2 fusion.71
  349.7 1.4 gather_fusion.1
  352.1 1.2 fusion.71
  357.4 1.4 gather_fusion.1
  359.8 1.2 fusion.71
  365.1 1.4 gather_fusion.1
  367.5 1.2 fusion.71
  372.8 1.4 gather_fusion.1
  375.2 1.2 fusion.71
  380.4 1.4 gather_fusion.1
  382.9 1.2 fusion.71
  388.1 1.4 gather_fusion.1
  390.6 1.2 fusion.71
  395.8 1.4 gather_fusion.1
  398.3 1.2 fusion.71
  403.5 1.4 gather_fusion.1
  406.0 1.2 fusion.71
  411.2 1.4 gather_fusion.1
  413.7 1.2 fusion.71
  418.9 1.4 gather_fusion.1
  421.3 1.2 fusion.71
  424.4 3.3 convolution_convert_fusion
  427.7 403.1 %reduce-scatter.2.cloned.1.call-done = bf16[512,256]{1,0:T(8,128)(2,1)} async-done(((bf16[512,2048]{1,0:T(8,128)(2,1)}), bf16[512,256]{1,0:T(8,128)(2,1)}) %reduce-scatter.2.cloned.1.call-update) | async-done | bytes 262160 | tf_op jit(solution)/shard_map/reduce_scatter | solution.py:187
  (307 shorter events, 92.1 us)
Async XLA Ops:
  7.2 11.3 %copy-start.1 = (s32[16]{0:T(128)S(1)}, s32[16]{0:T(128)}, u32[]{:S(2)}) copy-start(s32[16]{0:T(128)} %param.12) | copy-start | bytes 196
  7.2 36.6 %all-gather.5.cloned.1.call-start = ((), (), s32[]{:S(2)}) async-start(), calls=%async_computation.2 | async-start | bytes 2359296 | tf_op jit(solution)/shard_map/all_gather | solution.py:131
  10.4 31.8 %all-to-all-start = ((bf16[16,128,384]{1,2,0:T(8,128)(2,1)}), bf16[16,128,384]{1,2,0:T(8,128)(2,1)S(1)}, u32[]{:S(2)}, u32[]{:S(2)}) async-start(bf16[16,128,384]{1,2,0:T(8,128)(2,1)} %tile.2), calls=%async_computation | async-start | bytes 3145728 | tf_op jit(solution)/shard_map/all_to_all | solution.py:16
  18.4 72.8 %all-gather.7.cloned.1.call-start = ((), (), s32[]{:S(2)}) async-start(), calls=%async_computation.3 | async-start | bytes 2228224 | tf_op jit(solution)/shard_map/all_gather | solution.py:151
  43.8 3.8 copy-start
  47.6 245.9 %all-gather.9.cloned.1.call-start = ((), (), s32[]{:S(2)}) async-start(), calls=%async_computation.4 | async-start | bytes 35651584 | tf_op jit(solution)/shard_map/all_gather | solution.py:154
  96.9 327.5 %all-gather.11.cloned.1.call-start = ((), (), s32[]{:S(2)}) async-start(), calls=%async_computation.5 | async-start | bytes 1114112 | tf_op jit(solution)/shard_map/all_gather | solution.py:184
  97.5 733.4 %reduce-scatter.2.cloned.1.call-start = ((), (), s32[]{:S(2)}) async-start(), calls=%async_computation.6 | async-start | bytes 2359296 | tf_op jit(solution)/shard_map/reduce_scatter | solution.py:187
Sparse Core Ops, SparseCore 0:
  9.7 29.2 all-gather.4
  47.7 43.3 all-gather.6
  97.0 196.4 all-gather.8
  295.5 42.8 all-gather.10
  427.9 402.9 reduce-scatter.1
